TPU v7x, 32 devices: a whole 2x2x4 slice. The times are simulated.
32 devices in a mesh: rows: 16 (over z, y, x), grid: 2 (over core).
Axes of the slice: x: 2, y: 2, z: 4, core: 2. Of those that a mesh axis runs over, the one named last changes fastest.
Arguments:
- library: bfloat16 [8192, 4096], P('rows', 'grid'), may hold values from -6 to 6
- col_scale: float32 [4096], replicated, may hold values from 0.5 to 2
Outputs:
- updated: float32 [4096, 4096], P('rows', 'grid')
- reflectors: float32 [4096, 64], P('rows')
All inputs are finite; a program needn't handle non-finite values.
Results may differ from a plain program's by a relative error of at most 0.0003.
Values may be sent and summed in bfloat16 or wider, within the bound.
A program may use at most 128 MiB of HBM per device.

v0:
```python
import jax
import jax.numpy as jnp
from jax import lax
from jax.sharding import PartitionSpec as P

PANEL = 64


def broadcast(block, axis, source):
    block = jnp.where(lax.axis_index(axis) == source, block, jnp.zeros_like(block))
    return lax.psum(block, axis)


def reflect_panel(panel):
    size, width = panel.shape
    row_line = jnp.arange(size)
    col_line = jnp.arange(width)
    vectors = jnp.zeros((size, width), jnp.float32)
    factor = jnp.zeros((width, width), jnp.float32)

    def one_step(step, carry):
        work, vectors, factor = carry
        column = jnp.sum(jnp.where(col_line[None, :] == step, work, 0.0), axis=1)
        column = jnp.where(row_line >= step, column, 0.0)
        pivot = jnp.sum(jnp.where(row_line == step, column, 0.0))
        length = jnp.sqrt(jnp.sum(column * column))
        sign_factor = jnp.where(pivot >= 0.0, 1.0, -1.0)
        vector = column + jnp.where(row_line == step, sign_factor * length, 0.0)
        scale = 2.0 / jnp.sum(vector * vector)
        project = jnp.dot(vector, work, precision=lax.Precision.HIGHEST)
        work = work - scale * vector[:, None] * project[None, :]
        coupling = jnp.dot(vector, vectors, precision=lax.Precision.HIGHEST)
        column_t = -scale * jnp.dot(factor, coupling, precision=lax.Precision.HIGHEST)
        column_t = column_t + jnp.where(col_line == step, scale, 0.0)
        factor = jnp.where(col_line[None, :] == step, column_t[:, None], factor)
        vectors = jnp.where(col_line[None, :] == step, vector[:, None], vectors)
        return (work, vectors, factor)

    work, vectors, factor = lax.fori_loop(0, width, one_step, (panel, vectors, factor))
    return (vectors, factor)


def per_device(library, col_scale):
    rows_dev, col_block = library.shape
    count_rows = lax.axis_size("rows")
    count_grid = lax.axis_size("grid")
    columns = col_block * count_grid
    row_block = columns // count_rows
    total = rows_dev * count_rows
    grid_place = lax.axis_index("grid")
    rows_place = lax.axis_index("rows")
    own_scale = lax.dynamic_slice_in_dim(col_scale, grid_place * col_block, col_block)
    whole = lax.all_gather(library, "grid", axis=1, tiled=True)
    product = lax.dot_general(
        whole, library, (((0,), (0,)), ((), ())), preferred_element_type=jnp.float32
    )
    gram = lax.psum_scatter(
        product * (col_scale[:, None] * own_scale[None, :] / total),
        "rows",
        scatter_dimension=0,
        tiled=True,
    )
    head = gram[:, :PANEL]
    head = broadcast(head, "grid", 0)
    panel = lax.all_gather(head, "rows", axis=0, tiled=True)
    vectors, factor = reflect_panel(panel)
    own_vectors = lax.dynamic_slice_in_dim(vectors, rows_place * row_block, row_block, 0)
    partial_cross = jnp.dot(own_vectors.T, gram, precision=lax.Precision.HIGHEST)
    cross = lax.psum(partial_cross, "rows")
    mixed = jnp.dot(factor.T, cross, precision=lax.Precision.HIGHEST)
    updated = gram - jnp.dot(own_vectors, mixed, precision=lax.Precision.HIGHEST)
    return (updated, own_vectors)


def solution(mesh):
    return jax.shard_map(
        per_device,
        mesh=mesh,
        in_specs=(P("rows", "grid"), P()),
        out_specs=(P("rows", "grid"), P("rows", None)),
        check_vma=False,
    )
```

profile of v0, /device:TPU:0, one launch (start us, length us, event | category | flops | bytes accessed | tf_op | source)
XLA Modules:
  0.0 1997.8 jit_solution(2636637013112608751)
XLA Ops:
  8.0 17.9 all-gather.3.cloned.1.call-done
  26.0 17.6 multiply_multiply_fusion
  43.7 684.7 %reduce-scatter.2.cloned.1.call-done = f32[256,2048]{1,0:T(8,128)} async-done(((f32[4096,2048]{1,0:T(8,128)}), f32[256,2048]{1,0:T(8,128)}) %reduce-scatter.2.cloned.1.call-update) | async-done | bytes 2097168 | tf_op jit(solution)/shard_map/reduce_scatter | solution.py:57
  730.0 24.8 %all-reduce.3.cloned.1.call-done = f32[256,64]{1,0:T(8,128)} async-done(((f32[256,64]{1,0:T(8,128)}), f32[256,64]{1,0:T(8,128)}) %all-reduce.3.cloned.1.call-update) | async-done | bytes 65552 | tf_op jit(solution)/shard_map/psum | solution.py:11
  755.2 64.3 %all-gather.5.cloned.1.call-done = f32[4096,64]{1,0:T(8,128)} async-done(((f32[256,64]{1,0:T(8,128)}), f32[4096,64]{1,0:T(8,128)}) %all-gather.5.cloned.1.call-update) | async-done | bytes 1048592 | tf_op jit(solution)/shard_map/all_gather | solution.py:65
  819.4 1055.3 %while.19 = (s32[]{:T(128)}, f32[4096,64]{1,0:T(8,128)}, f32[4096,64]{1,0:T(8,128)}, f32[64,64]{1,0:T(8,128)S(1)}, s32[]{:T(128)}, /*index=5*/f32[]{:T(128)}, f32[]{:T(128)}, f32[]{:T(128)}, f32[]{:T(128)}, s32[]{:T(128)}) while((s32[]{:T(128)}, f32[4096,64]{1,0:T(8,128)}, f32[4096,64]{1,0:T(8,128)}, ...), condition=%wide.region_7.8_spmd.clone.clone, body=%wide.region_2.7_spmd.clone.clone.sunk | while | flops 8245573 | bytes 24332360 | solution.py:39
  827.6 3.9 multiply_subtract_fusion.2
  860.6 3.9 multiply_subtract_fusion.2
  877.2 3.9 multiply_subtract_fusion.2
  893.7 3.9 multiply_subtract_fusion.2
  910.2 3.9 multiply_subtract_fusion.2
  926.7 3.9 multiply_subtract_fusion.2
  943.2 3.9 multiply_subtract_fusion.2
  959.7 3.9 multiply_subtract_fusion.2
  976.3 3.9 multiply_subtract_fusion.2
  992.8 3.9 multiply_subtract_fusion.2
  1009.3 3.9 multiply_subtract_fusion.2
  1025.8 3.9 multiply_subtract_fusion.2
  1042.3 3.9 multiply_subtract_fusion.2
  1058.8 3.9 multiply_subtract_fusion.2
  1075.4 3.9 multiply_subtract_fusion.2
  1091.9 3.9 multiply_subtract_fusion.2
  1108.4 3.9 multiply_subtract_fusion.2
  1124.9 3.9 multiply_subtract_fusion.2
  1141.4 3.9 multiply_subtract_fusion.2
  1174.5 3.9 multiply_subtract_fusion.2
  1191.0 3.9 multiply_subtract_fusion.2
  1207.5 3.9 multiply_subtract_fusion.2
  1224.0 3.9 multiply_subtract_fusion.2
  1240.5 3.9 multiply_subtract_fusion.2
  1257.0 3.9 multiply_subtract_fusion.2
  1273.6 3.9 multiply_subtract_fusion.2
  1290.1 3.9 multiply_subtract_fusion.2
  1306.6 3.9 multiply_subtract_fusion.2
  1323.1 3.9 multiply_subtract_fusion.2
  1339.6 3.9 multiply_subtract_fusion.2
  1356.1 3.9 multiply_subtract_fusion.2
  1372.7 3.9 multiply_subtract_fusion.2
  1389.2 3.9 multiply_subtract_fusion.2
  1405.7 3.9 multiply_subtract_fusion.2
  1422.2 3.9 multiply_subtract_fusion.2
  1438.7 3.9 multiply_subtract_fusion.2
  1455.2 3.9 multiply_subtract_fusion.2
  1488.3 3.9 multiply_subtract_fusion.2
  1504.8 3.9 multiply_subtract_fusion.2
  1521.3 3.9 multiply_subtract_fusion.2
  1537.8 3.9 multiply_subtract_fusion.2
  1879.3 107.1 %all-reduce.5.cloned.1.call-done = f32[64,2048]{1,0:T(8,128)} async-done(((f32[64,2048]{1,0:T(8,128)}), f32[64,2048]{1,0:T(8,128)}) %all-reduce.5.cloned.1.call-update) | async-done | bytes 524304 | tf_op jit(solution)/shard_map/psum | solution.py:69
  (1138 shorter events, 767.4 us)
Async XLA Ops:
  7.2 18.8 copy-start.5
  7.2 18.8 all-gather.3.cloned.1.call-start
  7.9 720.5 %reduce-scatter.2.cloned.1.call-start = ((), (), s32[]{:S(2)}) async-start(), calls=%async_computation.2 | async-start | bytes 35651584 | tf_op jit(solution)/shard_map/reduce_scatter | solution.py:57
  43.6 711.2 %all-reduce.3.cloned.1.call-start = ((), (), s32[]{:S(2)}) async-start(), calls=%async_computation.3 | async-start | bytes 262144 | tf_op jit(solution)/shard_map/psum | solution.py:11
  730.0 89.4 %all-gather.5.cloned.1.call-start = ((), (), s32[]{:S(2)}) async-start(), calls=%async_computation.4 | async-start | bytes 2228224 | tf_op jit(solution)/shard_map/all_gather | solution.py:65
  754.9 1231.5 %all-reduce.5.cloned.1.call-start = ((), (), s32[]{:S(2)}) async-start(), calls=%async_computation.5 | async-start | bytes 1048576 | tf_op jit(solution)/shard_map/psum | solution.py:69
  834.2 8.8 copy-start
  850.7 8.8 copy-start
  867.2 8.8 copy-start
  883.7 8.8 copy-start
  900.3 8.8 copy-start
  916.8 8.8 copy-start
  933.3 8.8 copy-start
  949.8 8.8 copy-start
  966.3 8.8 copy-start
  982.8 8.8 copy-start
  999.4 8.8 copy-start
  1015.9 8.8 copy-start
  1032.4 8.8 copy-start
  1048.9 8.8 copy-start
  1065.4 8.8 copy-start
  1082.0 8.8 copy-start
  1098.5 8.8 copy-start
  1115.0 8.8 copy-start
  1148.0 8.8 copy-start
  1164.5 8.8 copy-start
  1181.1 8.8 copy-start
  1197.6 8.8 copy-start
  1214.1 8.8 copy-start
  1313.2 8.8 copy-start
  1329.7 8.8 copy-start
  1346.2 8.8 copy-start
  1362.7 8.8 copy-start
  1461.8 8.8 copy-start
  1478.4 8.8 copy-start
  1494.9 8.8 copy-start
  1511.4 8.8 copy-start
  1527.9 8.8 copy-start
  1627.0 8.8 copy-start
  1643.5 8.8 copy-start
  1660.0 8.8 copy-start
  1676.6 8.8 copy-start
  1775.7 8.8 copy-start
  1792.2 8.8 copy-start
  1808.7 8.8 copy-start
  1825.2 8.8 copy-start
  1841.7 8.8 copy-start
  1877.1 111.0 %copy-start.6 = (f32[256,64]{0,1:T(8,128)}, f32[256,64]{0,1:T(8,128)S(1)}, u32[]{:S(2)}) copy-start(f32[256,64]{0,1:T(8,128)S(1)} %constant_dynamic-slice_fusion) | copy-start | bytes 196612
  (217 other events, 632.0 us)
Sparse Core Ops, SparseCore 0:
  9.6 16.3 all-gather.2
  43.8 684.5 reduce-scatter.1
  731.3 23.5 all-reduce.2
  757.5 61.8 all-gather.4
  1879.5 106.9 all-reduce.4
where the time goes:
time: 2000 us
  waiting for transfers between devices  900 us (45%)
  other arithmetic  496 us (25%)
  matrix products  290 us (14%)
  local copies, waits for them, and re-layouts  158 us (8%)
  loops' own time  140 us (7%)
    reduce_scatter x1, waiting for transfers between devices, per_device(): lax.psum_scatter(product * (col_scale[:, None] * own_scale[None, :] / tot...  685 us
    sub x64, other arithmetic, one_step(): work = work - scale * vector[:, None] * project[None, :]  250 us
    dot_general x64, matrix products, one_step(): coupling = jnp.dot(vector, vectors, precision=lax.Precision.HIGHEST)  184 us
    while x512, local copies, waits for them, and re-layouts  156 us
    reduce_sum x64, other arithmetic, one_step(): column = jnp.sum(jnp.where(col_line[None, :] == step, work, 0.0), axis=1)  150 us
    another operation x1, loops' own time, reflect_panel(): lax.fori_loop(0, width, one_step, (panel, vectors, factor))  140 us
    psum x1, waiting for transfers between devices, per_device(): cross = lax.psum(partial_cross, 'rows')  107 us
    dot_general x64, matrix products, one_step(): project = jnp.dot(vector, work, precision=lax.Precision.HIGHEST)  72.2 us
  transfers between devices with their start and end apart: 5, of which 5 were waited for; matrix products, arithmetic and copies ran while one was open for 0% of the time, Pallas kernels for 0%

commit v1 on v0

v1 whole, which is shorter than its diff:
```python
import jax
import jax.numpy as jnp
from jax import lax
from jax.experimental import pallas as pl
from jax.experimental.pallas import tpu as pltpu
from jax.sharding import PartitionSpec as P

PANEL = 64
HIGH = lax.Precision.HIGHEST


def reflect_kernel(panel_ref, vectors_ref, weights_ref, work, inner, taus):
    width, size = panel_ref.shape
    lane = lax.broadcasted_iota(jnp.int32, (1, size), 1)
    work[...] = panel_ref[...]
    for base in range(0, width, 8):

        def one_step(step, carry, base=base):
            place = base + step
            row = work[pl.ds(place, 1), :]
            row = jnp.where(lane >= place, row, 0.0)
            pivot = jnp.sum(jnp.where(lane == place, row, 0.0), axis=1, keepdims=True)
            length = jnp.sqrt(jnp.sum(row * row, axis=1, keepdims=True))
            signed = jnp.where(pivot >= 0.0, length, -length)
            vector = row + jnp.where(lane == place, signed, 0.0)
            tau = 1.0 / (length * (length + jnp.abs(pivot)))
            rest = work[base:, :]
            project = jnp.sum(rest * vector, axis=1, keepdims=True)
            work[base:, :] = rest - (tau * project) * vector
            vectors_ref[pl.ds(place, 1), :] = vector
            taus[pl.ds(place, 1), :] = jnp.broadcast_to(tau, (1, 128))
            return carry

        lax.fori_loop(0, 8, one_step, 0)
    vectors = vectors_ref[...]
    inner[...] = lax.dot_general(
        vectors, vectors, (((1,), (1,)), ((), ())), precision=HIGH, preferred_element_type=jnp.float32
    )
    across = lax.broadcasted_iota(jnp.int32, (width, width), 1)
    down = lax.broadcasted_iota(jnp.int32, (width, 1), 0)

    def factor_step(place, factor):
        tau = taus[pl.ds(place, 1), 0:1]
        coupling = jnp.where(across < place, inner[pl.ds(place, 1), :] * factor, 0.0)
        column = -tau * jnp.sum(coupling, axis=1, keepdims=True)
        column = column + jnp.where(down == place, tau, 0.0)
        return jnp.where(across == place, column, factor)

    factor = lax.fori_loop(0, width, factor_step, jnp.zeros((width, width), jnp.float32))
    weights_ref[...] = lax.dot_general(
        factor, vectors, (((0,), (0,)), ((), ())), precision=HIGH, preferred_element_type=jnp.float32
    )


def reflect_panel(panel_t):
    width, size = panel_t.shape
    shape = jax.ShapeDtypeStruct((width, size), jnp.float32)
    return pl.pallas_call(
        reflect_kernel,
        out_shape=(shape, shape),
        in_specs=[pl.BlockSpec(memory_space=pltpu.VMEM)],
        out_specs=(pl.BlockSpec(memory_space=pltpu.VMEM),) * 2,
        scratch_shapes=[
            pltpu.VMEM((width, size), jnp.float32),
            pltpu.VMEM((width, width), jnp.float32),
            pltpu.VMEM((width, 128), jnp.float32),
        ],
        compiler_params=pltpu.CompilerParams(vmem_limit_bytes=16 << 20),
        cost_estimate=pl.CostEstimate(flops=20_000_000_000, bytes_accessed=100_000_000, transcendentals=0),
    )(panel_t)


def per_device(library, col_scale):
    rows_dev, col_block = library.shape
    count_rows = lax.axis_size("rows")
    count_grid = lax.axis_size("grid")
    columns = col_block * count_grid
    row_block = columns // count_rows
    total = rows_dev * count_rows
    near = 1
    while near * near < count_rows:
        near *= 2
    far = count_rows // near
    grid_place = lax.axis_index("grid")
    rows_place = lax.axis_index("rows")
    near_groups = [[f * near + n for n in range(near)] for f in range(far)]
    far_groups = [[f * near + n for f in range(far)] for n in range(near)]
    own_scale = lax.dynamic_slice_in_dim(col_scale, grid_place * col_block, col_block)

    head = lax.all_gather(library[:, :PANEL], "grid", axis=0)[0]
    panel_part = lax.dot_general(
        head, library, (((0,), (0,)), ((), ())), preferred_element_type=jnp.float32
    )
    panel_own = lax.psum(panel_part, "rows") * (col_scale[:PANEL, None] * own_scale[None, :] / total)
    panel_t = lax.all_gather(panel_own, "grid", axis=1, tiled=True)
    vectors, weights = reflect_panel(panel_t)

    whole = lax.all_gather(library, "rows", axis=0, tiled=True, axis_index_groups=near_groups)
    place = rows_place % near
    blocks = whole.reshape(near * rows_dev, far // count_grid, near, row_block)
    left = lax.dynamic_index_in_dim(blocks, place, 2, keepdims=False)
    left = lax.all_gather(left, "grid", axis=1, tiled=True).reshape(near * rows_dev, far * row_block)
    product = lax.dot_general(
        left, whole, (((0,), (0,)), ((), ())), preferred_element_type=jnp.float32
    )
    gram = lax.psum_scatter(
        product, "rows", scatter_dimension=0, tiled=True, axis_index_groups=far_groups
    )
    row_scale = lax.dynamic_slice_in_dim(col_scale, rows_place * row_block, row_block)

    scaled = weights * col_scale[None, :]
    scaled = lax.dynamic_slice_in_dim(scaled, grid_place * col_block, col_block, 1)
    wide = library.astype(jnp.float32)
    inner = lax.dot_general(scaled, wide, (((1,), (1,)), ((), ())), precision=HIGH)
    inner = lax.psum(inner, "grid")
    mixed = lax.psum(jnp.dot(inner, wide, precision=HIGH), "rows") * (own_scale[None, :] / total)
    own_vectors = lax.dynamic_slice_in_dim(vectors, rows_place * row_block, row_block, 1).T
    gram = gram * (row_scale[:, None] * own_scale[None, :] / total)
    updated = gram - jnp.dot(own_vectors, mixed, precision=HIGH)
    return (updated, own_vectors)


def solution(mesh):
    return jax.shard_map(
        per_device,
        mesh=mesh,
        in_specs=(P("rows", "grid"), P()),
        out_specs=(P("rows", "grid"), P("rows", None)),
        check_vma=False,
    )
```

time: 2000 us -> 537 us (0.27)
  other arithmetic: 496 us -> 1.98 us
  waiting for transfers between devices: 900 us -> 433 us
  matrix products: 290 us -> 28.3 us
  loops' own time: 140 us -> 0 us
  local copies, waits for them, and re-layouts: 158 us -> 18.7 us
  Pallas kernels: 0 us -> 37.7 us
    reduce_scatter x1, waiting for transfers between devices: 685 us -> 146 us  [per_device(): lax.psum_scatter(product, 'rows', scatter_dimension=0, tiled=True, axis_i...]
    dot_general x196 -> x5, matrix products: 290 us -> 28.3 us  [the longest x1 14.6 us: per_device(): lax.dot_general(left, whole, (((0,), (0,)), ((), ())), preferred_element_...]
    sub x64 -> x0, other arithmetic: 250 us -> none  [one_step(): work = work - scale * vector[:, None] * project[None, :]]
    reduce_sum x192 -> x0, other arithmetic: 238 us -> none  [the longest x64 150 us: one_step(): column = jnp.sum(jnp.where(col_line[None, :] == step, work, 0.0), axis=1)]
    while x513 -> x0, local copies, waits for them, and re-layouts: 158 us -> none
    another operation x1 -> x0, loops' own time: 140 us -> none  [reflect_panel(): lax.fori_loop(0, width, one_step, (panel, vectors, factor))]
    psum x2 -> x3, waiting for transfers between devices: 132 us -> 219 us  [the longest x1 111 us: per_device(): lax.psum(panel_part, 'rows')]
    pallas_call x0 -> x1, Pallas kernels: none -> 37.7 us  [reflect_panel(): pl.pallas_call(reflect_kernel, out_shape=(shape, shape), in_specs=[pl.Blo...]
  transfers between devices with their start and end apart: 5 -> 7, of which waited for: 5 -> 7; matrix products, arithmetic and copies ran while one was open for 0% -> 7% of each run, Pallas kernels for 0% -> 7%
where the time goes in v1:
time: 537 us; the launch traced here: 536 us
  waiting for transfers between devices  433 us (81%)
  Pallas kernels  37.7 us (7%)
  matrix products  28.3 us (5%)
  local copies, waits for them, and re-layouts  18.7 us (3%)
  between operations  14.2 us (3%)
    reduce_scatter x1, waiting for transfers between devices, per_device(): lax.psum_scatter(product, 'rows', scatter_dimension=0, tiled=True, axis_i...  146 us
    psum x1, waiting for transfers between devices, per_device(): lax.psum(panel_part, 'rows')  111 us
    psum x1, waiting for transfers between devices, per_device(): lax.psum(jnp.dot(inner, wide, precision=HIGH), 'rows')  94.3 us
    all_gather x1, waiting for transfers between devices, per_device(): lax.all_gather(library, 'rows', axis=0, tiled=True, axis_index_groups=nea...  49.6 us
    pallas_call x1, Pallas kernels, reflect_panel(): pl.pallas_call(reflect_kernel, out_shape=(shape, shape), in_specs=[pl.Blo...  37.7 us
    dot_general x1, matrix products, per_device(): lax.dot_general(left, whole, (((0,), (0,)), ((), ())), preferred_element_...  14.6 us
    all_gather x1, waiting for transfers between devices, per_device(): lax.all_gather(left, 'grid', axis=1, tiled=True)  13.2 us
    psum x1, waiting for transfers between devices, per_device(): inner = lax.psum(inner, 'grid')  13 us
  transfers between devices with their start and end apart: 7, of which 7 were waited for; matrix products, arithmetic and copies ran while one was open for 7% of the time, Pallas kernels for 7%

profile of v1, /device:TPU:0, one launch (start us, length us, event | category | flops | bytes accessed | tf_op | source)
XLA Modules:
  0.0 536.3 jit_solution(543041130638217511)
XLA Ops:
  7.2 0.0 copy-start.2
  7.2 0.0 slice-start
  7.2 0.0 all-reduce.4.cloned.1.call-start
  7.2 0.9 slice.9
  8.1 2.1 all-gather.1
  10.2 0.0 copy-start.1
  10.2 3.0 fusion.4
  13.3 0.0 all-reduce.4.cloned.1.call-update
  13.3 0.0 all-gather.8.cloned.1.call-start
  13.4 0.0 copy-done.2
  13.4 111.4 %all-reduce.4.cloned.1.call-done = f32[64,2048]{1,0:T(8,128)} async-done(((f32[64,2048]{1,0:T(8,128)}), f32[64,2048]{1,0:T(8,128)}) %all-reduce.4.cloned.1.call-update) | async-done | bytes 524304 | tf_op jit(solution)/shard_map/psum | solution.py:94
  124.8 0.0 slice-done
  124.8 2.0 multiply_multiply_fusion
  126.7 0.0 all-gather.8.cloned.1.call-update
  126.8 0.0 all-gather.6.cloned.1.call-start
  126.8 0.0 copy-done.1
  126.8 2.5 copy.5
  129.3 0.0 all-gather.6.cloned.1.call-update
  129.4 0.0 all-reduce.6.cloned.1.call-start
  129.4 5.5 %all-gather.8.cloned.1.call-done.panel_ref = f32[64,4096]{1,0:T(8,128)} async-done(((f32[64,2048]{1,0:T(8,128)}), f32[64,4096]{1,0:T(8,128)}) %all-gather.8.cloned.1.call-update) | async-done | bytes 1048592 | tf_op jit(solution)/shard_map/all_gather | solution.py:95
  134.9 0.0 copy-start
  134.9 1.2 copy-done
  136.1 37.7 %shard_map.41 = (f32[64,4096]{1,0:T(8,128)S(1)}, f32[64,4096]{1,0:T(8,128)S(1)}) custom-call(f32[64,4096]{1,0:T(8,128)S(1)} %copy-done), custom_call_target="tpu_custom_call" | custom-call | flops 20000000000 | bytes 100000000 | tf_op jit(solution)/shard_map/pallas_call | solution.py:58
  173.8 2.7 fusion
  176.5 0.0 all-reduce.6.cloned.1.call-update
  176.5 0.0 all-gather.10.cloned.1.call-start
  176.6 49.6 %all-gather.6.cloned.1.call-done = bf16[2048,2048]{0,1:T(8,128)(2,1)} async-done(((bf16[512,2048]{0,1:T(8,128)(2,1)}), bf16[2048,2048]{0,1:T(8,128)(2,1)}) %all-gather.6.cloned.1.call-update) | async-done | bytes 8388624 | tf_op jit(solution)/shard_map/all_gather | solution.py:98
  226.2 3.2 constant_dynamic-slice_fusion
  229.3 4.0 copy.6
  233.3 0.0 all-gather.10.cloned.1.call-update
  233.3 0.0 all-reduce.8.cloned.1.call-start
  233.4 13.0 %all-reduce.6.cloned.1.call-done = f32[64,512]{1,0:T(8,128)} async-done(((f32[64,512]{1,0:T(8,128)}), f32[64,512]{1,0:T(8,128)}) %all-reduce.6.cloned.1.call-update) | async-done | bytes 131088 | tf_op jit(solution)/shard_map/psum | solution.py:115
  246.4 2.9 fusion.10
  249.3 0.0 all-reduce.8.cloned.1.call-update
  249.3 0.2 reduce-scatter.2.cloned.1.call-start
  249.5 13.2 %all-gather.10.cloned.1.call-done = bf16[2048,4,1,256]{3,0,2,1:T(8,128)(2,1)} async-done(((bf16[2048,2,1,256]{3,0,2,1:T(8,128)(2,1)}), bf16[2048,4,1,256]{3,0,2,1:T(8,128)(2,1)}) %all-gather.10.cloned.1.call-update) | async-done | bytes 4194320 | tf_op jit(solution)/shard_map/all_gather | solution.py:102
  262.7 6.2 %copy.7 = bf16[2048,4,1,256]{0,3,1,2:T(8,128)(2,1)} copy(bf16[2048,4,1,256]{3,0,2,1:T(8,128)(2,1)} %all-gather.10.cloned.1.call-done) | data formatting | bytes 8388608 | tf_op jit(solution)/shard_map/all_gather | solution.py:102
  269.0 14.6 %fusion.9 = f32[1024,2048]{1,0:T(8,128)} fusion(bf16[2048,1024]{0,1:T(8,128)(2,1)} %bitcast.10, bf16[2048,2048]{0,1:T(8,128)(2,1)} %all-gather.6.cloned.1.call-done), kind=kOutput, calls=%fused_computation.15 | convolution fusion | flops 8589934592 | bytes 20971520 | tf_op jit(solution)/shard_map/dot_general | solution.py:103
  283.6 0.0 reduce-scatter.2.cloned.1.call-update
  283.6 0.1 dynamic_slice.17
  283.7 0.6 dynamic-slice_bitcast_fusion
  284.3 94.3 %all-reduce.8.cloned.1.call-done = f32[64,2048]{1,0:T(8,128)} async-done(((f32[64,2048]{1,0:T(8,128)}), f32[64,2048]{1,0:T(8,128)}) %all-reduce.8.cloned.1.call-update) | async-done | bytes 524304 | tf_op jit(solution)/shard_map/psum | solution.py:116
  378.6 145.8 %reduce-scatter.2.cloned.1.call-done = f32[256,2048]{1,0:T(8,128)} async-done(((f32[1024,2048]{1,0:T(8,128)}), f32[256,2048]{1,0:T(8,128)}) %reduce-scatter.2.cloned.1.call-update) | async-done | bytes 2097168 | tf_op jit(solution)/shard_map/reduce_scatter | solution.py:106
  524.4 5.1 convolution_subtract_fusion
  (1 shorter events, 0.0 us)
Async XLA Ops:
  7.2 6.2 %copy-start.2 = (f32[4096]{0:T(1024)S(1)}, f32[4096]{0:T(1024)}, u32[]{:S(2)}) copy-start(f32[4096]{0:T(1024)} %param.3) | copy-start | bytes 49156
  7.2 117.6 %slice-start = ((f32[4096]{0:T(1024)}), f32[64]{0:T(128)S(1)}, s32[]{:S(2)}) async-start(f32[4096]{0:T(1024)} %param.3), calls=%async_computation.8 | async-start | bytes 1024 | tf_op jit(solution)/shard_map/slice | solution.py:94
  7.2 117.6 %all-reduce.4.cloned.1.call-start = ((), (), s32[]{:S(2)}) async-start(), calls=%async_computation.3 | async-start | bytes 1048576 | tf_op jit(solution)/shard_map/psum | solution.py:94
  10.2 116.6 %copy-start.1 = (bf16[512,2048]{1,0:T(8,128)(2,1)S(1)}, bf16[512,2048]{1,0:T(8,128)(2,1)}, u32[]{:S(2)}) copy-start(bf16[512,2048]{1,0:T(8,128)(2,1)} %param.2) | copy-start | bytes 6291460
  13.3 121.6 %all-gather.8.cloned.1.call-start = ((), (), s32[]{:S(2)}) async-start(), calls=%async_computation.4 | async-start | bytes 1572864 | tf_op jit(solution)/shard_map/all_gather | solution.py:95
  126.8 99.4 %all-gather.6.cloned.1.call-start = ((), (), s32[]{:S(2)}) async-start(), calls=%async_computation.1 | async-start | bytes 10485760 | tf_op jit(solution)/shard_map/all_gather | solution.py:98
  129.4 117.0 %all-reduce.6.cloned.1.call-start = ((), (), s32[]{:S(2)}) async-start(), calls=%async_computation.5 | async-start | bytes 262144 | tf_op jit(solution)/shard_map/psum | solution.py:115
  134.9 1.2 copy-start
  176.5 86.2 %all-gather.10.cloned.1.call-start = ((), (), s32[]{:S(2)}) async-start(), calls=%async_computation.7 | async-start | bytes 6291456 | tf_op jit(solution)/shard_map/all_gather | solution.py:102
  233.3 145.3 %all-reduce.8.cloned.1.call-start = ((), (), s32[]{:S(2)}) async-start(), calls=%async_computation.6 | async-start | bytes 1048576 | tf_op jit(solution)/shard_map/psum | solution.py:116
  249.3 275.1 %reduce-scatter.2.cloned.1.call-start = ((), (), s32[]{:S(2)}) async-start(), calls=%async_computation.2 | async-start | bytes 10485760 | tf_op jit(solution)/shard_map/reduce_scatter | solution.py:106
Sparse Core Ops, SparseCore 0:
  13.7 110.9 all-reduce.3
  126.9 7.9 all-gather.7
  137.4 88.6 all-gather.5
  228.4 17.9 all-reduce.5
  247.8 14.8 all-gather.9
  269.1 109.4 all-reduce.7
  380.9 143.3 reduce-scatter.1

commit v2 on v1

--- a/solution.py
+++ b/solution.py
@@ -1,3 +1,5 @@
+import functools
+
 import jax
 import jax.numpy as jnp
 from jax import lax
@@ -9,10 +11,9 @@
 HIGH = lax.Precision.HIGHEST
 
 
-def reflect_kernel(panel_ref, vectors_ref, weights_ref, work, inner, taus):
-    width, size = panel_ref.shape
+def reflect(vectors_ref, weights_ref, work, inner, taus):
+    width, size = work.shape
     lane = lax.broadcasted_iota(jnp.int32, (1, size), 1)
-    work[...] = panel_ref[...]
     for base in range(0, width, 8):
 
         def one_step(step, carry, base=base):
@@ -52,22 +53,151 @@
     )
 
 
-def reflect_panel(panel_t):
-    width, size = panel_t.shape
-    shape = jax.ShapeDtypeStruct((width, size), jnp.float32)
+def remote(source, target, send, recv, place):
+    return pltpu.make_async_remote_copy(
+        src_ref=source, dst_ref=target, send_sem=send, recv_sem=recv,
+        device_id=place, device_id_type=pl.DeviceIdType.MESH,
+    )
+
+
+def sum_rows(count, part, landed, out, sems):
+    me, core = lax.axis_index("rows"), lax.axis_index("grid")
+    send, recv, send_back, recv_back = sems
+
+    def scatter(step):
+        peer = lax.rem(me + step, count)
+        return remote(part.at[peer], landed.at[step], send.at[step], recv.at[step], (peer, core))
+
+    def spread(step):
+        peer = lax.rem(me + step, count)
+        return remote(out.at[me], out.at[me], send_back.at[step], recv_back.at[step], (peer, core))
+
+    def arrival(step):
+        peer = lax.rem(me + count - step, count)
+        return remote(out.at[peer], out.at[peer], send_back.at[step], recv_back.at[step], (peer, core))
+
+    def loop(action):
+        def body(step, carry):
+            action(step)
+            return carry
+        lax.fori_loop(1, count, body, 0)
+
+    loop(lambda step: scatter(step).start())
+    loop(lambda step: scatter(step).wait_recv())
+    total = part[me]
+    for step in range(1, count):
+        total = total + landed[step]
+    out[me] = total
+    loop(lambda step: spread(step).start())
+    loop(lambda step: arrival(step).wait_recv())
+    loop(lambda step: scatter(step).wait_send())
+    loop(lambda step: spread(step).wait_send())
+
+
+def panel_kernel(
+    count, cores, part_ref, library_ref, scale_ref, vectors_ref, mixed_ref,
+    part, landed, gathered, part_two, landed_two, gathered_two, halves,
+    weights, work, inner, taus, row_sems, row_sems_two, core_sems, half_sems,
+):
+    me, core = lax.axis_index("rows"), lax.axis_index("grid")
+    width, block = part_ref.shape
+    per = width // count
+    barrier = pltpu.get_barrier_semaphore()
+
+    def greet(step, carry):
+        pl.semaphore_signal(
+            barrier, inc=1, device_id=(lax.rem(me + step, count), core), device_id_type=pl.DeviceIdType.MESH
+        )
+        return carry
+
+    lax.fori_loop(1, count, greet, 0)
+    for step in range(1, cores):
+        pl.semaphore_signal(
+            barrier, inc=1, device_id=(me, lax.rem(core + step, cores)), device_id_type=pl.DeviceIdType.MESH
+        )
+    for place in range(count):
+        part[place] = part_ref[place * per:(place + 1) * per, :]
+    pl.semaphore_wait(barrier, count + cores - 2)
+
+    sum_rows(count, part, landed, gathered.at[core], [row_sems.at[k] for k in range(4)])
+    shares = []
+    for step in range(1, cores):
+        peer = lax.rem(core + step, cores)
+        shares.append(
+            remote(gathered.at[core], gathered.at[core], core_sems.at[0, step], core_sems.at[1, step], (me, peer))
+        )
+        shares[-1].start()
+    for step in range(1, cores):
+        peer = lax.rem(core + cores - step, cores)
+        remote(
+            gathered.at[peer], gathered.at[peer], core_sems.at[0, step], core_sems.at[1, step], (me, peer)
+        ).wait_recv()
+    for share in shares:
+        share.wait_send()
+    for half in range(cores):
+        for place in range(count):
+            work[place * per:(place + 1) * per, half * block:(half + 1) * block] = gathered[half, place]
+
+    reflect(vectors_ref, weights, work, inner, taus)
+
+    step_cols = min(block, 512)
+    halves[0] = jnp.zeros_like(halves[0])
+    for start in range(0, block, step_cols):
+        cols = slice(start, start + step_cols)
+        own = weights[:, pl.ds(pl.multiple_of(core * block + start, 128), step_cols)] * scale_ref[:, cols]
+        halves[0] += lax.dot_general(
+            own, library_ref[:, cols].astype(jnp.float32), (((1,), (1,)), ((), ())),
+            precision=HIGH, preferred_element_type=jnp.float32,
+        )
+    shares = []
+    for step in range(1, cores):
+        peer = lax.rem(core + step, cores)
+        shares.append(
+            remote(halves.at[0], halves.at[step], half_sems.at[0, step], half_sems.at[1, step], (me, peer))
+        )
+        shares[-1].start()
+    for share in shares:
+        share.wait()
+    summed = halves[0]
+    for step in range(1, cores):
+        summed = summed + halves[step]
+    for start in range(0, block, step_cols):
+        cols = slice(start, start + step_cols)
+        chunk = jnp.dot(
+            summed, library_ref[:, cols].astype(jnp.float32), precision=HIGH, preferred_element_type=jnp.float32
+        )
+        for place in range(count):
+            part_two[place, :, cols] = chunk[place * per:(place + 1) * per, :]
+    sum_rows(count, part_two, landed_two, gathered_two, [row_sems_two.at[k] for k in range(4)])
+    for place in range(count):
+        mixed_ref[place * per:(place + 1) * per, :] = gathered_two[place] * scale_ref[...]
+
+
+def panel_chain(part, library, scale, count, cores):
+    width, block = part.shape
+    rows_dev = library.shape[0]
+    per = width // count
+    size = block * cores
+    real = jnp.float32
+    slices = pltpu.VMEM((count, per, block), real)
     return pl.pallas_call(
-        reflect_kernel,
-        out_shape=(shape, shape),
-        in_specs=[pl.BlockSpec(memory_space=pltpu.VMEM)],
+        functools.partial(panel_kernel, count, cores),
+        out_shape=(jax.ShapeDtypeStruct((width, size), real), jax.ShapeDtypeStruct((width, block), real)),
+        in_specs=[pl.BlockSpec(memory_space=pltpu.VMEM)] * 3,
         out_specs=(pl.BlockSpec(memory_space=pltpu.VMEM),) * 2,
         scratch_shapes=[
-            pltpu.VMEM((width, size), jnp.float32),
-            pltpu.VMEM((width, width), jnp.float32),
-            pltpu.VMEM((width, 128), jnp.float32),
+            slices, slices, pltpu.VMEM((cores, count, per, block), real),
+            slices, slices, slices, pltpu.VMEM((cores, width, rows_dev), real),
+            pltpu.VMEM((width, size), real), pltpu.VMEM((width, size), real),
+            pltpu.VMEM((width, width), real), pltpu.VMEM((width, 128), real),
+            pltpu.SemaphoreType.DMA((4, count)), pltpu.SemaphoreType.DMA((4, count)),
+            pltpu.SemaphoreType.DMA((2, cores)), pltpu.SemaphoreType.DMA((2, cores)),
         ],
-        compiler_params=pltpu.CompilerParams(vmem_limit_bytes=16 << 20),
-        cost_estimate=pl.CostEstimate(flops=20_000_000_000, bytes_accessed=100_000_000, transcendentals=0),
-    )(panel_t)
+        compiler_params=pltpu.CompilerParams(
+            vmem_limit_bytes=32 << 20, collective_id=0, has_side_effects=True
+        ),
+        cost_estimate=pl.CostEstimate(flops=20_000_000_000, bytes_accessed=200_000_000, transcendentals=0),
+    )(part, library, scale)
 
 
 def per_device(library, col_scale):
@@ -91,9 +221,9 @@
     panel_part = lax.dot_general(
         head, library, (((0,), (0,)), ((), ())), preferred_element_type=jnp.float32
     )
-    panel_own = lax.psum(panel_part, "rows") * (col_scale[:PANEL, None] * own_scale[None, :] / total)
-    panel_t = lax.all_gather(panel_own, "grid", axis=1, tiled=True)
-    vectors, weights = reflect_panel(panel_t)
+    panel_part = panel_part * (col_scale[:PANEL, None] * own_scale[None, :] / total)
+    vectors, mixed = panel_chain(panel_part, library, own_scale[None, :], count_rows, count_grid)
+    mixed = mixed / total
 
     whole = lax.all_gather(library, "rows", axis=0, tiled=True, axis_index_groups=near_groups)
     place = rows_place % near
@@ -108,12 +238,6 @@
     )
     row_scale = lax.dynamic_slice_in_dim(col_scale, rows_place * row_block, row_block)
 
-    scaled = weights * col_scale[None, :]
-    scaled = lax.dynamic_slice_in_dim(scaled, grid_place * col_block, col_block, 1)
-    wide = library.astype(jnp.float32)
-    inner = lax.dot_general(scaled, wide, (((1,), (1,)), ((), ())), precision=HIGH)
-    inner = lax.psum(inner, "grid")
-    mixed = lax.psum(jnp.dot(inner, wide, precision=HIGH), "rows") * (own_scale[None, :] / total)
     own_vectors = lax.dynamic_slice_in_dim(vectors, rows_place * row_block, row_block, 1).T
     gram = gram * (row_scale[:, None] * own_scale[None, :] / total)
     updated = gram - jnp.dot(own_vectors, mixed, precision=HIGH)

time: 537 us -> 341 us (0.64)
  waiting for transfers between devices: 433 us -> 142 us
  Pallas kernels: 37.7 us -> 142 us
  matrix products: 28.3 us -> 20 us
    psum x3 -> x0, waiting for transfers between devices: 219 us -> none  [the longest x1 111 us: per_device(): lax.psum(panel_part, 'rows')]
    reduce_scatter x1, waiting for transfers between devices: 146 us -> 37.6 us  [per_device(): lax.psum_scatter(product, 'rows', scatter_dimension=0, tiled=True, axis_i...]
    pallas_call x1, Pallas kernels: 37.7 us -> 142 us  [panel_chain(): pl.pallas_call(functools.partial(panel_kernel, count, cores), out_shape=(...]
    all_gather x1, waiting for transfers between devices: 49.6 us -> 90.3 us  [per_device(): lax.all_gather(library, 'rows', axis=0, tiled=True, axis_index_groups=nea...]
    dot_general x2 -> x0, matrix products: 5.6 us -> none  [the longest x1 2.9 us: per_device(): jnp.dot(inner, wide, precision=HIGH)]
    all_gather x1 -> x0, waiting for transfers between devices: 5.48 us -> none  [per_device(): panel_t = lax.all_gather(panel_own, 'grid', axis=1, tiled=True)]
  transfers between devices with their start and end apart: 7 -> 3, of which waited for: 7 -> 3; matrix products, arithmetic and copies ran while one was open for 7% -> 0% of each run, Pallas kernels for 7% -> 42%
where the time goes in v2:
time: 341 us; the launch traced here: 337 us
  waiting for transfers between devices  142 us (42%)
  Pallas kernels  142 us (42%)
  matrix products  20 us (6%)
  local copies, waits for them, and re-layouts  16.9 us (5%)
  between operations  13.8 us (4%)
    pallas_call x1, Pallas kernels, panel_chain(): pl.pallas_call(functools.partial(panel_kernel, count, cores), out_shape=(...  142 us
    all_gather x1, waiting for transfers between devices, per_device(): lax.all_gather(library, 'rows', axis=0, tiled=True, axis_index_groups=nea...  90.3 us
    reduce_scatter x1, waiting for transfers between devices, per_device(): lax.psum_scatter(product, 'rows', scatter_dimension=0, tiled=True, axis_i...  37.6 us
    dot_general x1, matrix products, per_device(): lax.dot_general(left, whole, (((0,), (0,)), ((), ())), preferred_element_...  14.6 us
    all_gather x1, waiting for transfers between devices, per_device(): lax.all_gather(left, 'grid', axis=1, tiled=True)  13.8 us
  transfers between devices with their start and end apart: 3, of which 3 were waited for; matrix products, arithmetic and copies ran while one was open for 0% of the time, Pallas kernels for 42%

profile of v2, /device:TPU:0, one launch (start us, length us, event | category | flops | bytes accessed | tf_op | source)
XLA Modules:
  0.0 336.6 jit_solution(17821806328252398654)
XLA Ops:
  7.2 0.0 all-gather.5.cloned.1.call-start
  7.2 3.9 %copy.5 = bf16[512,2048]{0,1:T(8,128)(2,1)} copy(bf16[512,2048]{1,0:T(8,128)(2,1)} %library_ref.1) | data formatting | bytes 4194304 | tf_op args[0]
  11.1 0.0 all-gather.5.cloned.1.call-update
  11.2 0.0 all-gather.7.cloned.1.call-start
  11.2 90.3 %all-gather.5.cloned.1.call-done = bf16[2048,2048]{0,1:T(8,128)(2,1)} async-done(((bf16[512,2048]{0,1:T(8,128)(2,1)}), bf16[2048,2048]{0,1:T(8,128)(2,1)}) %all-gather.5.cloned.1.call-update) | async-done | bytes 8388624 | tf_op jit(solution)/shard_map/all_gather | solution.py:228
  101.5 1.7 constant_dynamic-slice_fusion
  103.2 2.5 copy.6
  105.7 0.0 all-gather.7.cloned.1.call-update
  105.7 0.0 reduce-scatter.2.cloned.1.call-start
  105.8 13.8 %all-gather.7.cloned.1.call-done = bf16[2048,4,1,256]{3,0,2,1:T(8,128)(2,1)} async-done(((bf16[2048,2,1,256]{3,0,2,1:T(8,128)(2,1)}), bf16[2048,4,1,256]{3,0,2,1:T(8,128)(2,1)}) %all-gather.7.cloned.1.call-update) | async-done | bytes 4194320 | tf_op jit(solution)/shard_map/all_gather | solution.py:232
  119.6 6.2 %copy.7 = bf16[2048,4,1,256]{0,3,1,2:T(8,128)(2,1)} copy(bf16[2048,4,1,256]{3,0,2,1:T(8,128)(2,1)} %all-gather.7.cloned.1.call-done) | data formatting | bytes 8388608 | tf_op jit(solution)/shard_map/all_gather | solution.py:232
  125.8 14.6 %fusion.6 = f32[1024,2048]{1,0:T(8,128)} fusion(bf16[2048,1024]{0,1:T(8,128)(2,1)} %bitcast.9, bf16[2048,2048]{0,1:T(8,128)(2,1)} %all-gather.5.cloned.1.call-done), kind=kOutput, calls=%fused_computation.10 | convolution fusion | flops 8589934592 | bytes 20971520 | tf_op jit(solution)/shard_map/dot_general | solution.py:233
  140.4 0.0 copy-start.2
  140.4 0.0 slice-start
  140.4 0.0 copy-start
  140.4 0.0 slice-start.1
  140.4 0.0 reduce-scatter.2.cloned.1.call-update
  140.5 0.7 copy-done.2
  141.1 0.1 dynamic_slice.14
  141.2 0.1 slice-done
  141.3 2.2 all-gather.1
  143.5 0.0 copy-done
  143.5 0.0 slice-done.1
  143.5 0.5 convolution_multiply_fusion.part_ref
  144.0 141.9 %shard_map.41 = (f32[64,4096]{1,0:T(8,128)S(1)}, f32[64,2048]{1,0:T(8,128)S(1)}) custom-call(f32[64,2048]{1,0:T(8,128)S(1)} %convolution_multiply_fusion.part_ref, bf16[512,2048]{1,0:T(8,128)(2,1)S(1)} %copy-done, f32[1,2048]{1,0:T(1,128)S(1)} %bitcast.8), custom_call_target="tpu_custom_call" | custom-call | flops 20000000000 | bytes 200000000 | tf_op jit(solution)/shard_map/pallas_call | solution.py:183
  285.9 0.0 copy-start.1
  286.0 1.0 copy-done.1
  286.9 0.6 dynamic-slice_bitcast_fusion
  287.5 37.6 %reduce-scatter.2.cloned.1.call-done = f32[256,2048]{1,0:T(8,128)} async-done(((f32[1024,2048]{1,0:T(8,128)}), f32[256,2048]{1,0:T(8,128)}) %reduce-scatter.2.cloned.1.call-update) | async-done | bytes 2097168 | tf_op jit(solution)/shard_map/reduce_scatter | solution.py:236
  325.2 4.9 %convolution_subtract_fusion = f32[256,2048]{1,0:T(8,128)} fusion(f32[256,2048]{1,0:T(8,128)} %reduce-scatter.2.cloned.1.call-done, f32[2048]{0:T(1024)S(1)} %dynamic_slice.15, f32[256]{0:T(256)S(1)} %dynamic_slice.14, f32[64,2048]{1,0:T(8,128)S(1)} %get-tuple-element.5, f32[64,4096]{1,0:T(8,128)} %copy-done.1, s32[]{:T(128)S(6)} %select_n.20), kind=kOutput, calls=%fused_computation | convolution fusion | flops 404881408 | bytes 4793348 | tf_op jit(solution)/shard_map/dot_general | solution.py:243
  (1 shorter events, 0.0 us)
Async XLA Ops:
  7.2 94.3 %all-gather.5.cloned.1.call-start = ((), (), s32[]{:S(2)}) async-start(), calls=%async_computation.1 | async-start | bytes 10485760 | tf_op jit(solution)/shard_map/all_gather | solution.py:228
  11.2 108.4 %all-gather.7.cloned.1.call-start = ((), (), s32[]{:S(2)}) async-start(), calls=%async_computation.3 | async-start | bytes 6291456 | tf_op jit(solution)/shard_map/all_gather | solution.py:232
  105.7 219.4 %reduce-scatter.2.cloned.1.call-start = ((), (), s32[]{:S(2)}) async-start(), calls=%async_computation.2 | async-start | bytes 10485760 | tf_op jit(solution)/shard_map/reduce_scatter | solution.py:236
  140.4 0.7 copy-start.2
  140.4 0.9 slice-start
  140.4 3.1 copy-start
  140.4 3.1 slice-start.1
  285.9 1.0 copy-start.1
Sparse Core Ops, SparseCore 0:
  11.3 90.1 all-gather.4
  105.9 13.6 all-gather.6
  140.6 184.5 reduce-scatter.1

commit v3 on v2

--- a/solution.py
+++ b/solution.py
@@ -95,9 +95,10 @@
 
 
 def panel_kernel(
-    count, cores, part_ref, library_ref, scale_ref, vectors_ref, mixed_ref,
+    count, cores, near, aligned, part_ref, library_ref, scale_ref, vectors_ref, mixed_ref, whole_ref, left_ref,
     part, landed, gathered, part_two, landed_two, gathered_two, halves,
     weights, work, inner, taus, row_sems, row_sems_two, core_sems, half_sems,
+    near_sems, own_sem, side_sems, left_sems,
 ):
     me, core = lax.axis_index("rows"), lax.axis_index("grid")
     width, block = part_ref.shape
@@ -118,6 +119,26 @@
     for place in range(count):
         part[place] = part_ref[place * per:(place + 1) * per, :]
     pl.semaphore_wait(barrier, count + cores - 2)
+
+    place_near = lax.rem(me, near)
+    first = me - place_near
+
+    def to_peer(step):
+        peer = lax.rem(place_near + step, near)
+        return remote(
+            library_ref, whole_ref.at[place_near], near_sems.at[0, step], near_sems.at[1, step], (first + peer, core)
+        )
+
+    def from_peer(step):
+        peer = lax.rem(place_near + near - step, near)
+        return remote(
+            library_ref, whole_ref.at[peer], near_sems.at[0, step], near_sems.at[1, step], (first + peer, core)
+        )
+
+    keep = pltpu.make_async_copy(library_ref, whole_ref.at[place_near], own_sem)
+    keep.start()
+    for step in range(1, near):
+        to_peer(step).start()
 
     sum_rows(count, part, landed, gathered.at[core], [row_sems.at[k] for k in range(4)])
     shares = []
@@ -140,6 +161,27 @@
 
     reflect(vectors_ref, weights, work, inner, taus)
 
+    keep.wait()
+    for step in range(1, near):
+        from_peer(step).wait_recv()
+        to_peer(step).wait_send()
+    moves = []
+    if aligned:
+        far = count // near
+        row_block = block * cores // count
+        for piece in range(far // cores):
+            offset = pl.multiple_of((piece * near + place_near) * row_block, 128)
+            source = whole_ref.at[:, :, pl.ds(offset, row_block)]
+            target = left_ref.at[core, piece]
+            moves.append(pltpu.make_async_copy(source, target, left_sems.at[piece]))
+            moves[-1].start()
+            for step in range(1, cores):
+                peer = lax.rem(core + step, cores)
+                moves.append(
+                    remote(source, target, side_sems.at[0, step, piece], side_sems.at[1, step, piece], (me, peer))
+                )
+                moves[-1].start()
+
     step_cols = min(block, 512)
     halves[0] = jnp.zeros_like(halves[0])
     for start in range(0, block, step_cols):
@@ -171,20 +213,30 @@
     sum_rows(count, part_two, landed_two, gathered_two, [row_sems_two.at[k] for k in range(4)])
     for place in range(count):
         mixed_ref[place * per:(place + 1) * per, :] = gathered_two[place] * scale_ref[...]
-
-
-def panel_chain(part, library, scale, count, cores):
+    for move in moves:
+        move.wait()
+
+
+def panel_chain(part, library, scale, count, cores, near):
     width, block = part.shape
     rows_dev = library.shape[0]
     per = width // count
     size = block * cores
     real = jnp.float32
     slices = pltpu.VMEM((count, per, block), real)
+    row_block = size // count
+    aligned = row_block % 128 == 0
+    pieces = count // near // cores
     return pl.pallas_call(
-        functools.partial(panel_kernel, count, cores),
-        out_shape=(jax.ShapeDtypeStruct((width, size), real), jax.ShapeDtypeStruct((width, block), real)),
+        functools.partial(panel_kernel, count, cores, near, aligned),
+        out_shape=(
+            jax.ShapeDtypeStruct((width, size), real),
+            jax.ShapeDtypeStruct((width, block), real),
+            jax.ShapeDtypeStruct((near, rows_dev, block), jnp.bfloat16),
+            jax.ShapeDtypeStruct((cores, pieces, near, rows_dev, row_block), jnp.bfloat16),
+        ),
         in_specs=[pl.BlockSpec(memory_space=pltpu.VMEM)] * 3,
-        out_specs=(pl.BlockSpec(memory_space=pltpu.VMEM),) * 2,
+        out_specs=(pl.BlockSpec(memory_space=pltpu.VMEM),) * 2 + (pl.BlockSpec(memory_space=pltpu.HBM),) * 2,
         scratch_shapes=[
             slices, slices, pltpu.VMEM((cores, count, per, block), real),
             slices, slices, slices, pltpu.VMEM((cores, width, rows_dev), real),
@@ -192,6 +244,8 @@
             pltpu.VMEM((width, width), real), pltpu.VMEM((width, 128), real),
             pltpu.SemaphoreType.DMA((4, count)), pltpu.SemaphoreType.DMA((4, count)),
             pltpu.SemaphoreType.DMA((2, cores)), pltpu.SemaphoreType.DMA((2, cores)),
+            pltpu.SemaphoreType.DMA((2, near)), pltpu.SemaphoreType.DMA(()),
+            pltpu.SemaphoreType.DMA((2, cores, pieces)), pltpu.SemaphoreType.DMA((pieces,)),
         ],
         compiler_params=pltpu.CompilerParams(
             vmem_limit_bytes=32 << 20, collective_id=0, has_side_effects=True
@@ -213,7 +267,6 @@
     far = count_rows // near
     grid_place = lax.axis_index("grid")
     rows_place = lax.axis_index("rows")
-    near_groups = [[f * near + n for n in range(near)] for f in range(far)]
     far_groups = [[f * near + n for f in range(far)] for n in range(near)]
     own_scale = lax.dynamic_slice_in_dim(col_scale, grid_place * col_block, col_block)
 
@@ -222,17 +275,22 @@
         head, library, (((0,), (0,)), ((), ())), preferred_element_type=jnp.float32
     )
     panel_part = panel_part * (col_scale[:PANEL, None] * own_scale[None, :] / total)
-    vectors, mixed = panel_chain(panel_part, library, own_scale[None, :], count_rows, count_grid)
+    vectors, mixed, whole, left = panel_chain(
+        panel_part, library, own_scale[None, :], count_rows, count_grid, near
+    )
     mixed = mixed / total
 
-    whole = lax.all_gather(library, "rows", axis=0, tiled=True, axis_index_groups=near_groups)
-    place = rows_place % near
-    blocks = whole.reshape(near * rows_dev, far // count_grid, near, row_block)
-    left = lax.dynamic_index_in_dim(blocks, place, 2, keepdims=False)
-    left = lax.all_gather(left, "grid", axis=1, tiled=True).reshape(near * rows_dev, far * row_block)
+    samples = near * rows_dev
+    whole = whole.reshape(samples, col_block)
+    if row_block % 128:
+        blocks = whole.reshape(samples, far // count_grid, near, row_block)
+        left = lax.dynamic_index_in_dim(blocks, rows_place % near, 2, keepdims=False)
+        left = lax.all_gather(left, "grid", axis=1, tiled=True)
+    else:
+        left = left.reshape(far, samples, row_block).transpose(1, 0, 2)
     product = lax.dot_general(
         left, whole, (((0,), (0,)), ((), ())), preferred_element_type=jnp.float32
-    )
+    ).reshape(far * row_block, col_block)
     gram = lax.psum_scatter(
         product, "rows", scatter_dimension=0, tiled=True, axis_index_groups=far_groups
     )

time: 341 us -> 388 us (1.14); the launches traced: 337 us -> 388 us
  Pallas kernels: 142 us -> 186 us
  waiting for transfers between devices: 142 us -> 147 us
    reduce_scatter x1, waiting for transfers between devices: 37.6 us -> 147 us  [per_device(): lax.psum_scatter(product, 'rows', scatter_dimension=0, tiled=True, axis_i...]
    all_gather x2 -> x0, waiting for transfers between devices: 104 us -> none  [the longest x1 90.3 us: per_device(): lax.all_gather(library, 'rows', axis=0, tiled=True, axis_index_groups=nea...]
    pallas_call x1, Pallas kernels: 142 us -> 186 us  [panel_chain(): pl.pallas_call(functools.partial(panel_kernel, count, cores, near, aligne...]
    reshape x0 -> x1, local copies, waits for them, and re-layouts: none -> 6.27 us  [per_device(): left = left.reshape(far, samples, row_block).transpose(1, 0, 2)]
    all_gather x1 -> x0, local copies, waits for them, and re-layouts: 6.24 us -> none  [per_device(): lax.all_gather(left, 'grid', axis=1, tiled=True)]
    dynamic_slice x2 -> x0, local copies, waits for them, and re-layouts: 4.22 us -> none  [per_device(): left = lax.dynamic_index_in_dim(blocks, place, 2, keepdims=False)]
  transfers between devices with their start and end apart: 3 -> 1, of which waited for: 3 -> 1; matrix products, arithmetic and copies ran while one was open for 0% -> 1% of each run, Pallas kernels for 42% -> 0%
where the time goes in v3:
time: 388 us
  Pallas kernels  186 us (48%)
  waiting for transfers between devices  147 us (38%)
  matrix products  21.4 us (6%)
  local copies, waits for them, and re-layouts  17.1 us (4%)
  between operations  14.1 us (4%)
    pallas_call x1, Pallas kernels, panel_chain(): pl.pallas_call(functools.partial(panel_kernel, count, cores, near, aligne...  186 us
    reduce_scatter x1, waiting for transfers between devices, per_device(): lax.psum_scatter(product, 'rows', scatter_dimension=0, tiled=True, axis_i...  147 us
    dot_general x1, matrix products, per_device(): lax.dot_general(left, whole, (((0,), (0,)), ((), ())), preferred_element_...  14.4 us
  transfers between devices with their start and end apart: 1, of which 1 were waited for; matrix products, arithmetic and copies ran while one was open for 1% of the time, Pallas kernels for 0%

profile of v3, /device:TPU:0, one launch (start us, length us, event | category | flops | bytes accessed | tf_op | source)
XLA Modules:
  0.0 387.6 jit_solution(2068284527815645409)
XLA Ops:
  7.2 0.0 copy-start.1
  7.2 0.0 reduce-scatter.2.cloned.1.call-start
  7.2 0.8 slice.11
  8.1 0.7 dynamic_slice.9
  8.8 0.9 slice.9
  9.7 2.1 all-gather
  11.8 2.1 convolution_multiply_fusion.part_ref
  13.9 0.0 copy-done.1
  13.9 186.1 %shard_map.41 = (f32[64,4096]{1,0:T(8,128)S(1)}, f32[64,2048]{1,0:T(8,128)S(1)}, bf16[4,512,2048]{2,1,0:T(8,128)(2,1)S(1)}, bf16[2,2,4,512,256]{4,3,2,1,0:T(8,128)(2,1)S(1)}) custom-call(f32[64,2048]{1,0:T(8,128)S(1)} %convolution_multiply_fusion.part_ref, bf16[512,2048]{1,0:T(8,128)(2,1)S(1)} %copy-done.1, f32[1,2048]{1,0:T(1,128)S(1)} %bitcast.12), custom_call_target="tpu_custom_call" | custom-call | flops 20000000000 | bytes 200000000 | tf_op jit(solution)/shard_map/pallas_call | solution.py:230
  200.0 0.0 copy-start
  200.0 1.9 copy-done
  202.0 0.0 copy-start.2
  202.0 1.0 copy-done.2
  203.0 0.0 copy-start.3
  203.0 3.2 copy-done.3
  206.2 6.3 %copy.4 = bf16[4,2048,256]{1,2,0:T(8,128)(2,1)} copy(bf16[4,2048,256]{2,1,0:T(8,128)(2,1)} %bitcast.11) | data formatting | bytes 8388608 | tf_op jit(solution)/shard_map/reshape | solution.py:290
  212.5 14.4 %fusion.6 = f32[1024,2048]{1,0:T(8,128)} fusion(bf16[1024,2048]{1,0:T(8,128)(2,1)} %bitcast.14, bf16[2048,2048]{1,0:T(8,128)(2,1)} %bitcast.13), kind=kOutput, calls=%fused_computation.9 | convolution fusion | flops 8589934592 | bytes 20971520 | tf_op jit(solution)/shard_map/dot_general | solution.py:291
  226.8 0.0 reduce-scatter.2.cloned.1.call-update
  226.9 0.8 dynamic_slice.10
  227.6 1.5 dynamic-slice_bitcast_fusion
  229.1 146.7 %reduce-scatter.2.cloned.1.call-done = f32[256,2048]{1,0:T(8,128)} async-done(((f32[1024,2048]{1,0:T(8,128)}), f32[256,2048]{1,0:T(8,128)}) %reduce-scatter.2.cloned.1.call-update) | async-done | bytes 2097168 | tf_op jit(solution)/shard_map/reduce_scatter | solution.py:294
  375.8 4.9 %convolution_subtract_fusion = f32[256,2048]{1,0:T(8,128)} fusion(f32[256,2048]{1,0:T(8,128)} %reduce-scatter.2.cloned.1.call-done, f32[2048]{0:T(1024)S(1)} %dynamic_slice.9, f32[256]{0:T(256)S(1)} %dynamic_slice.10, f32[64,2048]{1,0:T(8,128)S(1)} %get-tuple-element.9, f32[64,4096]{1,0:T(8,128)} %copy-done.2, s32[]{:T(128)S(6)} %select_n.8), kind=kOutput, calls=%fused_computation | convolution fusion | flops 404881408 | bytes 4793348 | tf_op jit(solution)/shard_map/dot_general | solution.py:301
Async XLA Ops:
  7.2 6.7 %copy-start.1 = (bf16[512,2048]{1,0:T(8,128)(2,1)S(1)}, bf16[512,2048]{1,0:T(8,128)(2,1)}, u32[]{:S(2)}) copy-start(bf16[512,2048]{1,0:T(8,128)(2,1)} %library_ref.1) | copy-start | bytes 6291460
  7.2 368.6 %reduce-scatter.2.cloned.1.call-start = ((), (), s32[]{:S(2)}) async-start(), calls=%async_computation.1 | async-start | bytes 10485760 | tf_op jit(solution)/shard_map/reduce_scatter | solution.py:294
  200.0 2.0 copy-start
  202.0 1.0 copy-start.2
  203.0 3.2 copy-start.3
Sparse Core Ops, SparseCore 0:
  227.0 148.7 reduce-scatter.1

commit v4 on v2

--- a/solution.py
+++ b/solution.py
@@ -226,6 +226,7 @@
     mixed = mixed / total
 
     whole = lax.all_gather(library, "rows", axis=0, tiled=True, axis_index_groups=near_groups)
+    whole, vectors, mixed = lax.optimization_barrier((whole, vectors, mixed))
     place = rows_place % near
     blocks = whole.reshape(near * rows_dev, far // count_grid, near, row_block)
     left = lax.dynamic_index_in_dim(blocks, place, 2, keepdims=False)

time: 341 us -> 318 us (0.933); the launches traced: 337 us -> 317 us
  Pallas kernels: 142 us -> 104 us
  waiting for transfers between devices: 142 us -> 160 us
    reduce_scatter x1, waiting for transfers between devices: 37.6 us -> 145 us  [per_device(): lax.psum_scatter(product, 'rows', scatter_dimension=0, tiled=True, axis_i...]
    all_gather x1, waiting for transfers between devices: 90.3 us -> 1.5 us  [per_device(): lax.all_gather(library, 'rows', axis=0, tiled=True, axis_index_groups=nea...]
    pallas_call x1, Pallas kernels: 142 us -> 104 us  [panel_chain(): pl.pallas_call(functools.partial(panel_kernel, count, cores), out_shape=(...]
  transfers between devices with their start and end apart: 3 -> 3, of which waited for: 3 -> 3; matrix products, arithmetic and copies ran while one was open for 0% -> 1% of each run, Pallas kernels for 42% -> 33%
where the time goes in v4:
time: 318 us; the launch traced here: 317 us
  waiting for transfers between devices  160 us (50%)
  Pallas kernels  104 us (33%)
  matrix products  20 us (6%)
  local copies, waits for them, and re-layouts  15.9 us (5%)
  between operations  13.8 us (4%)
    reduce_scatter x1, waiting for transfers between devices, per_device(): lax.psum_scatter(product, 'rows', scatter_dimension=0, tiled=True, axis_i...  145 us
    pallas_call x1, Pallas kernels, panel_chain(): pl.pallas_call(functools.partial(panel_kernel, count, cores), out_shape=(...  104 us
    dot_general x1, matrix products, per_device(): lax.dot_general(left, whole, (((0,), (0,)), ((), ())), preferred_element_...  14.6 us
    all_gather x1, waiting for transfers between devices, per_device(): lax.all_gather(left, 'grid', axis=1, tiled=True)  13.7 us
  transfers between devices with their start and end apart: 3, of which 3 were waited for; matrix products, arithmetic and copies ran while one was open for 1% of the time, Pallas kernels for 33%

profile of v4, /device:TPU:0, one launch (start us, length us, event | category | flops | bytes accessed | tf_op | source)
XLA Modules:
  0.0 317.4 jit_solution(2707258302847370676)
XLA Ops:
  7.2 0.0 all-gather.5.cloned.1.call-start
  7.2 3.9 %copy.5 = bf16[512,2048]{0,1:T(8,128)(2,1)} copy(bf16[512,2048]{1,0:T(8,128)(2,1)} %library_ref.1) | data formatting | bytes 4194304 | tf_op args[0]
  11.1 0.0 copy-start.2
  11.1 0.0 slice-start
  11.1 0.0 copy-start
  11.1 0.0 slice-start.1
  11.1 0.0 all-gather.5.cloned.1.call-update
  11.2 0.0 all-gather.7.cloned.1.call-start
  11.2 0.6 copy-done.2
  11.9 0.2 slice-done
  12.1 2.1 all-gather
  14.1 0.0 copy-done
  14.1 0.0 slice-done.1
  14.1 0.5 convolution_multiply_fusion.part_ref
  14.6 104.2 %shard_map.41 = (f32[64,4096]{1,0:T(8,128)S(1)}, f32[64,2048]{1,0:T(8,128)S(1)}) custom-call(f32[64,2048]{1,0:T(8,128)S(1)} %convolution_multiply_fusion.part_ref, bf16[512,2048]{1,0:T(8,128)(2,1)S(1)} %copy-done, f32[1,2048]{1,0:T(1,128)S(1)} %bitcast.9), custom_call_target="tpu_custom_call" | custom-call | flops 20000000000 | bytes 200000000 | tf_op jit(solution)/shard_map/pallas_call | solution.py:183
  118.8 0.8 broadcast_multiply_fusion
  119.6 1.5 all-gather.5.cloned.1.call-done
  121.1 1.7 constant_dynamic-slice_fusion
  122.9 2.5 copy.6
  125.4 0.0 all-gather.7.cloned.1.call-update
  125.4 0.2 reduce-scatter.2.cloned.1.call-start
  125.6 13.7 %all-gather.7.cloned.1.call-done = bf16[2048,4,1,256]{3,0,2,1:T(8,128)(2,1)} async-done(((bf16[2048,2,1,256]{3,0,2,1:T(8,128)(2,1)}), bf16[2048,4,1,256]{3,0,2,1:T(8,128)(2,1)}) %all-gather.7.cloned.1.call-update) | async-done | bytes 4194320 | tf_op jit(solution)/shard_map/all_gather | solution.py:233
  139.3 6.2 %copy.7 = bf16[2048,4,1,256]{0,3,1,2:T(8,128)(2,1)} copy(bf16[2048,4,1,256]{3,0,2,1:T(8,128)(2,1)} %all-gather.7.cloned.1.call-done) | data formatting | bytes 8388608 | tf_op jit(solution)/shard_map/all_gather | solution.py:233
  145.6 14.6 %fusion.3 = f32[1024,2048]{1,0:T(8,128)} fusion(bf16[2048,1024]{0,1:T(8,128)(2,1)} %bitcast.10, bf16[2048,2048]{0,1:T(8,128)(2,1)} %all-gather.5.cloned.1.call-done), kind=kOutput, calls=%fused_computation.8 | convolution fusion | flops 8589934592 | bytes 20971520 | tf_op jit(solution)/shard_map/dot_general | solution.py:234
  160.2 0.0 copy-start.1
  160.2 0.0 reduce-scatter.2.cloned.1.call-update
  160.2 0.1 dynamic_slice.15
  160.3 0.6 dynamic-slice_bitcast_fusion
  160.9 145.1 %reduce-scatter.2.cloned.1.call-done = f32[256,2048]{1,0:T(8,128)} async-done(((f32[1024,2048]{1,0:T(8,128)}), f32[256,2048]{1,0:T(8,128)}) %reduce-scatter.2.cloned.1.call-update) | async-done | bytes 2097168 | tf_op jit(solution)/shard_map/reduce_scatter | solution.py:237
  306.0 0.0 copy-done.1
  306.0 4.9 %convolution_subtract_fusion = f32[256,2048]{1,0:T(8,128)} fusion(f32[64,2048]{1,0:T(8,128)S(1)} %copy-done.1, f32[256,2048]{1,0:T(8,128)} %reduce-scatter.2.cloned.1.call-done, f32[2048]{0:T(1024)S(1)} %dynamic_slice.13, f32[256]{0:T(256)S(1)} %dynamic_slice.15, f32[64,4096]{1,0:T(8,128)S(1)} %get-tuple-element.10, s32[]{:T(128)S(6)} %select_n.21), kind=kOutput, calls=%fused_computation | convolution fusion | flops 404750336 | bytes 4793348 | tf_op jit(solution)/shard_map/dot_general | solution.py:244
  (1 shorter events, 0.0 us)
Async XLA Ops:
  7.2 114.0 %all-gather.5.cloned.1.call-start = ((), (), s32[]{:S(2)}) async-start(), calls=%async_computation.1 | async-start | bytes 10485760 | tf_op jit(solution)/shard_map/all_gather | solution.py:228
  11.1 0.7 copy-start.2
  11.1 0.9 slice-start
  11.1 3.0 copy-start
  11.1 3.0 slice-start.1
  11.2 128.2 %all-gather.7.cloned.1.call-start = ((), (), s32[]{:S(2)}) async-start(), calls=%async_computation.3 | async-start | bytes 6291456 | tf_op jit(solution)/shard_map/all_gather | solution.py:233
  125.4 180.6 %reduce-scatter.2.cloned.1.call-start = ((), (), s32[]{:S(2)}) async-start(), calls=%async_computation.2 | async-start | bytes 10485760 | tf_op jit(solution)/shard_map/reduce_scatter | solution.py:237
  160.2 145.8 %copy-start.1 = (f32[64,2048]{1,0:T(8,128)S(1)}, f32[64,2048]{1,0:T(8,128)}, u32[]{:S(2)}) copy-start(f32[64,2048]{1,0:T(8,128)} %broadcast_multiply_fusion) | copy-start | bytes 1572868
Sparse Core Ops, SparseCore 0:
  11.3 109.8 all-gather.4
  125.5 13.7 all-gather.6
  160.3 145.6 reduce-scatter.1

commit v5 on v4

--- a/solution.py
+++ b/solution.py
@@ -228,11 +228,12 @@
     whole = lax.all_gather(library, "rows", axis=0, tiled=True, axis_index_groups=near_groups)
     whole, vectors, mixed = lax.optimization_barrier((whole, vectors, mixed))
     place = rows_place % near
-    blocks = whole.reshape(near * rows_dev, far // count_grid, near, row_block)
-    left = lax.dynamic_index_in_dim(blocks, place, 2, keepdims=False)
-    left = lax.all_gather(left, "grid", axis=1, tiled=True).reshape(near * rows_dev, far * row_block)
+    blocks = whole.T.reshape(far // count_grid, near, row_block, near * rows_dev)
+    left = lax.dynamic_index_in_dim(blocks, place, 1, keepdims=False)
+    left = left.reshape(far // count_grid * row_block, near * rows_dev)
+    left = lax.all_gather(left, "grid", axis=0, tiled=True)
     product = lax.dot_general(
-        left, whole, (((0,), (0,)), ((), ())), preferred_element_type=jnp.float32
+        left, whole, (((1,), (0,)), ((), ())), preferred_element_type=jnp.float32
     )
     gram = lax.psum_scatter(
         product, "rows", scatter_dimension=0, tiled=True, axis_index_groups=far_groups

time: 318 us -> 310 us (0.975)
  local copies, waits for them, and re-layouts: 15.9 us -> 8.62 us
    all_gather x1 -> x0, local copies, waits for them, and re-layouts: 6.24 us -> none  [per_device(): lax.all_gather(left, 'grid', axis=1, tiled=True)]
  transfers between devices with their start and end apart: 3 -> 3, of which waited for: 3 -> 3; matrix products, arithmetic and copies ran while one was open for 1% -> 0% of each run, Pallas kernels for 33% -> 34%
where the time goes in v5:
time: 310 us
  waiting for transfers between devices  161 us (52%)
  Pallas kernels  104 us (34%)
  matrix products  19.9 us (6%)
  between operations  13.8 us (4%)
  local copies, waits for them, and re-layouts  8.62 us (3%)
    reduce_scatter x1, waiting for transfers between devices, per_device(): lax.psum_scatter(product, 'rows', scatter_dimension=0, tiled=True, axis_i...  145 us
    pallas_call x1, Pallas kernels, panel_chain(): pl.pallas_call(functools.partial(panel_kernel, count, cores), out_shape=(...  104 us
    dot_general x1, matrix products, per_device(): lax.dot_general(left, whole, (((1,), (0,)), ((), ())), preferred_element_...  14.5 us
    all_gather x1, waiting for transfers between devices, per_device(): left = lax.all_gather(left, 'grid', axis=0, tiled=True)  13.7 us
  transfers between devices with their start and end apart: 3, of which 3 were waited for; matrix products, arithmetic and copies ran while one was open for 0% of the time, Pallas kernels for 34%

profile of v5, /device:TPU:0, one launch (start us, length us, event | category | flops | bytes accessed | tf_op | source)
XLA Modules:
  0.0 310.0 jit_solution(5353770337615580263)
XLA Ops:
  7.2 0.0 all-gather.4.cloned.1.call-start
  7.2 3.9 %copy.4 = bf16[512,2048]{0,1:T(8,128)(2,1)} copy(bf16[512,2048]{1,0:T(8,128)(2,1)} %library_ref.1) | data formatting | bytes 4194304 | tf_op args[0]
  11.1 0.0 copy-start.1
  11.1 0.0 slice-start
  11.1 0.0 copy-start
  11.1 0.0 slice-start.1
  11.1 0.0 all-gather.4.cloned.1.call-update
  11.2 0.0 all-gather.6.cloned.1.call-start
  11.2 0.6 copy-done.1
  11.9 0.2 slice-done
  12.1 2.1 all-gather
  14.1 0.0 copy-done
  14.1 0.0 slice-done.1
  14.1 0.5 convolution_multiply_fusion.part_ref
  14.6 104.2 %shard_map.41 = (f32[64,4096]{1,0:T(8,128)S(1)}, f32[64,2048]{1,0:T(8,128)S(1)}) custom-call(f32[64,2048]{1,0:T(8,128)S(1)} %convolution_multiply_fusion.part_ref, bf16[512,2048]{1,0:T(8,128)(2,1)S(1)} %copy-done, f32[1,2048]{1,0:T(1,128)S(1)} %bitcast.11), custom_call_target="tpu_custom_call" | custom-call | flops 20000000000 | bytes 200000000 | tf_op jit(solution)/shard_map/pallas_call | solution.py:183
  118.9 2.3 all-gather.4.cloned.1.call-done
  121.1 3.2 %constant_dynamic-slice_fusion = bf16[2,1,256,2048]{3,2,1,0:T(8,128)(2,1)} fusion(bf16[2,4,256,2048]{3,2,1,0:T(8,128)(2,1)} %bitcast.13, s32[]{:T(128)S(6)} %select_n.20), kind=kLoop, calls=%fused_computation.7 | loop fusion | bytes 4194308 | tf_op jit(solution)/shard_map/jit(dynamic_index_in_dim)/dynamic_slice | solution.py:232
  124.3 0.0 all-gather.6.cloned.1.call-update
  124.3 0.2 reduce-scatter.2.cloned.1.call-start
  124.6 13.7 %all-gather.6.cloned.1.call-done = bf16[1024,2048]{1,0:T(8,128)(2,1)} async-done(((bf16[512,2048]{1,0:T(8,128)(2,1)}), bf16[1024,2048]{1,0:T(8,128)(2,1)}) %all-gather.6.cloned.1.call-update) | async-done | bytes 4194320 | tf_op jit(solution)/shard_map/all_gather | solution.py:234
  138.3 14.5 %fusion.3 = f32[1024,2048]{1,0:T(8,128)} fusion(bf16[1024,2048]{1,0:T(8,128)(2,1)} %all-gather.6.cloned.1.call-done, bf16[2048,2048]{0,1:T(8,128)(2,1)} %all-gather.4.cloned.1.call-done), kind=kOutput, calls=%fused_computation.8 | convolution fusion | flops 8589934592 | bytes 20971520 | tf_op jit(solution)/shard_map/dot_general | solution.py:235
  152.8 0.0 reduce-scatter.2.cloned.1.call-update
  152.8 0.1 dynamic_slice.15
  152.9 0.6 dynamic-slice_bitcast_fusion
  153.5 145.1 %reduce-scatter.2.cloned.1.call-done = f32[256,2048]{1,0:T(8,128)} async-done(((f32[1024,2048]{1,0:T(8,128)}), f32[256,2048]{1,0:T(8,128)}) %reduce-scatter.2.cloned.1.call-update) | async-done | bytes 2097168 | tf_op jit(solution)/shard_map/reduce_scatter | solution.py:238
  298.6 4.9 %convolution_subtract_fusion = f32[256,2048]{1,0:T(8,128)} fusion(f32[64,2048]{1,0:T(8,128)S(1)} %broadcast_multiply_fusion, f32[256,2048]{1,0:T(8,128)} %reduce-scatter.2.cloned.1.call-done, f32[2048]{0:T(1024)S(1)} %dynamic_slice.13, f32[256]{0:T(256)S(1)} %dynamic_slice.15, f32[64,4096]{1,0:T(8,128)S(1)} %get-tuple-element.10, s32[]{:T(128)S(6)} %select_n.21), kind=kOutput, calls=%fused_computation | convolution fusion | flops 404750336 | bytes 4793348 | tf_op jit(solution)/shard_map/dot_general | solution.py:245
  (2 shorter events, 0.0 us)
Async XLA Ops:
  7.2 114.0 %all-gather.4.cloned.1.call-start = ((), (), s32[]{:S(2)}) async-start(), calls=%async_computation.1 | async-start | bytes 10485760 | tf_op jit(solution)/shard_map/all_gather | solution.py:228
  11.1 0.7 copy-start.1
  11.1 0.9 slice-start
  11.1 3.0 copy-start
  11.1 3.0 slice-start.1
  11.2 127.1 %all-gather.6.cloned.1.call-start = ((), (), s32[]{:S(2)}) async-start(), calls=%async_computation.2 | async-start | bytes 6291456 | tf_op jit(solution)/shard_map/all_gather | solution.py:234
  124.3 174.3 %reduce-scatter.2.cloned.1.call-start = ((), (), s32[]{:S(2)}) async-start(), calls=%async_computation.3 | async-start | bytes 10485760 | tf_op jit(solution)/shard_map/reduce_scatter | solution.py:238
Sparse Core Ops, SparseCore 0:
  11.3 109.8 all-gather.3
  124.5 13.7 all-gather.5
  152.9 145.6 reduce-scatter.1
